TPU v7x, 256 devices: a whole 4x4x8 slice. The times are simulated.
256 devices in a mesh: occ: 16 (over x_hi, y, core), ao: 16 (over x_lo, z).
Axes of the slice: x: 4 (x_hi: 2, x_lo: 2; x = x_hi * 2 + x_lo), y: 4, z: 8, core: 2. Of those that a mesh axis runs over, the one named last changes fastest.
Arguments:
- coef: bfloat16 [8192, 16], P('ao', 'occ'), may hold values from -0.25 to 0.25
- half_ints: bfloat16 [16, 1024, 8192], P('occ', None, 'ao'), may hold values from -0.5 to 0.5
- metric_inv: bfloat16 [64, 128, 128], replicated, may hold values from -1 to 2, as said below
- dom_blocks: int32 [16, 8], P('occ'), may hold values from 0 to 63, as said below
- dom_len: int32 [16], P('occ'), may hold values from 2 to 8
Outputs:
- exchange_k: float32 [8192, 8192], P('ao', 'occ')
- fit_density: float32 [8192], replicated
Inputs may be any that keep to these rules, and one draw needn't show every extreme that they name: `dom_blocks`: each row holds 8 different block numbers. `metric_inv`: full rank blocks.
All inputs are finite; a program needn't handle non-finite values.
Results may differ from a plain program's by a relative error of at most 0.0055.
Values may be sent and summed in bfloat16 or wider, within the bound.
A program may use at most 128 MiB of HBM per device.

v0:
```python
import jax
import jax.numpy as jnp
from jax import lax
from jax.sharding import PartitionSpec as P


def sent_to_all(x, axis):
    copies = jnp.broadcast_to(x, (lax.axis_size(axis), *x.shape))
    return lax.all_to_all(copies, axis, split_axis=0, concat_axis=0, tiled=True)


def over_copies(x, axis):
    everything = sent_to_all(x, axis)
    return jnp.sum(everything, axis=0)


def on_device(coef, half_ints, metric_inv, dom_blocks, dom_len):
    lmo_count, domain, ao_rows = half_ints.shape
    block = metric_inv.shape[1]
    slots = domain // block
    fit_blocks = metric_inv.shape[0]
    metric_rows = metric_inv[dom_blocks]
    raw_ints = half_ints.reshape(lmo_count, slots, block, ao_rows)
    fitted = jnp.einsum(
        "isab,isbm->isam", metric_rows, raw_ints, preferred_element_type=jnp.float32
    )
    live_slots = jnp.arange(slots, dtype=jnp.int32)[None, :] < dom_len[:, None]
    fitted = jnp.where(live_slots[:, :, None, None], fitted, 0.0)
    fitted = fitted.reshape(lmo_count, domain, ao_rows).astype(jnp.bfloat16)
    pair_part = jnp.einsum("ipm,mi->ip", fitted, coef, preferred_element_type=jnp.float32)
    one_hot = (
        dom_blocks[:, :, None] == jnp.arange(fit_blocks, dtype=jnp.int32)[None, None, :]
    ).astype(jnp.float32)
    pair_sum = over_copies(pair_part, "ao")
    local_density = jnp.einsum("isf,isr->fr", one_hot, pair_sum.reshape(lmo_count, slots, block))
    density = over_copies(local_density, "occ")
    density = density.reshape(fit_blocks * block)
    partial_value = jnp.einsum(
        "ipm,ipn->mn",
        fitted,
        lax.all_gather(fitted, "ao", axis=2, tiled=True),
        preferred_element_type=jnp.float32,
    )
    exchange_k = lax.psum_scatter(partial_value, "occ", scatter_dimension=1, tiled=True)
    return (exchange_k, density)


def solution(mesh):
    in_specs = (P("ao", "occ"), P("occ", None, "ao"), P(), P("occ", None), P("occ"))
    out_specs = (P("ao", "occ"), P())
    return jax.shard_map(
        on_device, mesh=mesh, in_specs=in_specs, out_specs=out_specs, check_vma=False
    )
```

profile of v0, /device:TPU:1, one launch (start us, length us, event | category | flops | bytes accessed | tf_op | source)
XLA Modules:
  0.0 376.6 jit_solution(9049975364195060182)
XLA Ops:
  7.2 0.0 copy-start
  7.2 0.0 all-gather.2.cloned.1.call-start
  8.0 0.7 fusion.7
  8.7 0.1 copy-done
  8.8 0.6 gather_fusion
  9.4 2.6 select_convert_fusion
  12.0 0.0 all-gather.2.cloned.1.call-update
  12.0 0.0 reduce-scatter.2.cloned.1.call-start
  12.1 189.1 %all-gather.2.cloned.1.call-done = bf16[1,1024,8192]{2,1,0:T(8,128)(2,1)} async-done(((bf16[1,1024,512]{2,1,0:T(8,128)(2,1)}), bf16[1,1024,8192]{2,1,0:T(8,128)(2,1)}) %all-gather.2.cloned.1.call-update) | async-done | bytes 16777232 | tf_op jit(solution)/shard_map/all_gather | solution.py:41
  201.2 16.0 %fusion = f32[512,8192]{1,0:T(8,128)} fusion(bf16[1024,512]{1,0:T(8,128)(2,1)} %bitcast.25, bf16[1,1024,8192]{2,1,0:T(8,128)(2,1)} %all-gather.2.cloned.1.call-done), kind=kOutput, calls=%fused_computation.1 | convolution fusion | flops 8589934592 | bytes 34603008 | tf_op jit(solution)/shard_map/ipm,ipn->mn/dot_general | solution.py:38
  217.2 0.0 copy-start.1
  217.2 0.0 copy-start.2
  217.2 0.0 copy-start.3
  217.2 0.0 reduce-scatter.2.cloned.1.call-update
  217.2 1.2 copy-done.1
  218.4 0.0 copy-done.2
  218.4 0.4 fusion.8
  218.8 0.1 broadcast_in_dim.29
  218.8 11.4 %all_to_all.10 = f32[16,1,1024]{2,1,0:T(1,128)S(1)} all-to-all(f32[16,1,1024]{2,1,0:T(1,128)S(1)} %broadcast_in_dim.29), channel_id=1, replica_groups=mesh['occ'=16,'ao'=16] {'ao'}, dimensions={0} | all-to-all | bytes 131072 | tf_op jit(solution)/shard_map/all_to_all | solution.py:9
  230.2 0.1 reduce_sum.18
  230.3 0.0 copy-done.3
  230.3 0.3 fusion.2
  230.6 19.6 %all_to_all.11 = f32[16,64,128]{2,1,0:T(8,128)S(1)} all-to-all(f32[16,64,128]{2,1,0:T(8,128)S(1)} %broadcast_in_dim.30), channel_id=1, replica_groups=mesh['occ'=16,'ao'=16] {'occ'}, dimensions={0} | all-to-all | bytes 1048576 | tf_op jit(solution)/shard_map/all_to_all | solution.py:9
  250.2 0.6 reduce_sum.19
  250.9 118.9 %reduce-scatter.2.cloned.1.call-done = f32[512,512]{1,0:T(8,128)} async-done(((f32[512,8192]{1,0:T(8,128)}), f32[512,512]{1,0:T(8,128)}) %reduce-scatter.2.cloned.1.call-update) | async-done | bytes 1048592 | tf_op jit(solution)/shard_map/reduce_scatter | solution.py:44
  (3 shorter events, 0.1 us)
Async XLA Ops:
  7.2 1.6 copy-start
  7.2 194.0 %all-gather.2.cloned.1.call-start = ((), (), s32[]{:S(2)}) async-start(), calls=%async_computation.3 | async-start | bytes 17825792 | tf_op jit(solution)/shard_map/all_gather | solution.py:41
  12.0 357.7 %reduce-scatter.2.cloned.1.call-start = ((), (), s32[]{:S(2)}) async-start(), calls=%async_computation.4 | async-start | bytes 17825792 | tf_op jit(solution)/shard_map/reduce_scatter | solution.py:44
  217.2 1.2 copy-start.1
  217.2 1.2 copy-start.2
  217.2 13.1 %copy-start.3 = (s32[1,8]{1,0:T(1,128)S(1)}, s32[1,8]{1,0:T(1,128)}, u32[]{:S(2)}) copy-start(s32[1,8]{1,0:T(1,128)} %param.8) | copy-start | bytes 100
Sparse Core Ops, SparseCore 0:
  12.2 189.0 all-gather.1
  217.3 152.3 reduce-scatter.1
where the time goes:
time: 377 us
  waiting for transfers between devices  308 us (82%)
  blocking collectives  31 us (8%)
  matrix products  19.2 us (5%)
  between operations  14.9 us (4%)
    all_gather x1, waiting for transfers between devices, on_device(): lax.all_gather(fitted, 'ao', axis=2, tiled=True)  189 us
    reduce_scatter x1, waiting for transfers between devices, on_device(): lax.psum_scatter(partial_value, 'occ', scatter_dimension=1, tiled=True)  119 us
    all_to_all x2, blocking collectives, sent_to_all(): return lax.all_to_all(copies, axis, split_axis=0, concat_axis=0, tiled=True)  31 us
    dot_general x1, matrix products, on_device(): jnp.einsum('ipm,ipn->mn', fitted, lax.all_gather(fitted, 'ao', axis=2, ti...  16 us
  transfers between devices with their start and end apart: 2, of which 2 were waited for; matrix products, arithmetic and copies ran while one was open for 0% of the time, Pallas kernels for 0%

commit v1 on v0

--- a/solution.py
+++ b/solution.py
@@ -38,7 +38,9 @@
     partial_value = jnp.einsum(
         "ipm,ipn->mn",
         fitted,
-        lax.all_gather(fitted, "ao", axis=2, tiled=True),
+        jnp.concatenate(
+            lax.all_to_all(jnp.stack([fitted] * lax.axis_size("ao")), "ao", 0, 0), axis=2
+        ),
         preferred_element_type=jnp.float32,
     )
     exchange_k = lax.psum_scatter(partial_value, "occ", scatter_dimension=1, tiled=True)

time: 377 us -> 566 us (1.50)
  blocking collectives: 31 us -> 406 us
  waiting for transfers between devices: 308 us -> 119 us
    all_to_all x0 -> x1, blocking collectives: none -> 372 us  [on_device(): lax.all_to_all(jnp.stack([fitted] * lax.axis_size('ao')), 'ao', 0, 0)]
    all_gather x1 -> x0, waiting for transfers between devices: 189 us -> none  [on_device(): lax.all_gather(fitted, 'ao', axis=2, tiled=True)]
  transfers between devices with their start and end apart: 2 -> 1, of which waited for: 2 -> 1; matrix products, arithmetic and copies ran while one was open for 0% -> 0% of each run, Pallas kernels for 0% -> 0%
where the time goes in v1:
time: 566 us
  blocking collectives  406 us (72%)
  waiting for transfers between devices  119 us (21%)
  matrix products  18 us (3%)
  between operations  14.7 us (3%)
  local copies, waits for them, and re-layouts  6.6 us (1%)
    all_to_all x1, blocking collectives, on_device(): lax.all_to_all(jnp.stack([fitted] * lax.axis_size('ao')), 'ao', 0, 0)  372 us
    reduce_scatter x1, waiting for transfers between devices, on_device(): lax.psum_scatter(partial_value, 'occ', scatter_dimension=1, tiled=True)  119 us
    all_to_all x2, blocking collectives, sent_to_all(): return lax.all_to_all(copies, axis, split_axis=0, concat_axis=0, tiled=True)  33.5 us
    dot_general x1, matrix products, on_device(): jnp.einsum('ipm,ipn->mn', fitted, jnp.concatenate(lax.all_to_all(jnp.stac...  15.7 us
  transfers between devices with their start and end apart: 1, of which 1 were waited for; matrix products, arithmetic and copies ran while one was open for 0% of the time, Pallas kernels for 0%

profile of v1, /device:TPU:1, one launch (start us, length us, event | category | flops | bytes accessed | tf_op | source)
XLA Modules:
  0.0 565.8 jit_solution(4408570215491477101)
XLA Ops:
  7.2 0.0 copy-start
  7.2 0.0 reduce-scatter.2.cloned.1.call-start
  7.2 0.8 fusion.5
  8.7 0.1 copy-done
  8.8 0.6 gather_fusion
  9.4 1.6 select_convert_fusion
  11.0 1.3 copy.12
  12.3 3.9 stack.2
  16.2 372.0 %all_to_all.15 = bf16[16,1,1024,512]{2,3,1,0:T(8,128)(2,1)} all-to-all(bf16[16,1,1024,512]{2,3,1,0:T(8,128)(2,1)S(1)} %stack.2), channel_id=1, replica_groups=mesh['occ'=16,'ao'=16] {'ao'}, dimensions={0} | all-to-all | bytes 33554432 | tf_op jit(solution)/shard_map/all_to_all | solution.py:42
  388.2 15.7 %fusion.6 = f32[512,8192]{1,0:T(8,128)} fusion(bf16[1024,512]{1,0:T(8,128)(2,1)S(1)} %bitcast.28, bf16[1024,8192]{0,1:T(8,128)(2,1)} %bitcast.26), kind=kOutput, calls=%fused_computation.11 | convolution fusion | flops 8589934592 | bytes 34603008 | tf_op jit(solution)/shard_map/ipm,ipn->mn/dot_general | solution.py:38
  403.9 0.0 copy-start.1
  403.9 0.0 copy-start.2
  403.9 0.0 reduce-scatter.2.cloned.1.call-update
  403.9 0.7 copy-done.1
  404.6 0.4 fusion.7
  404.9 0.1 broadcast_in_dim.29
  405.0 13.2 %all_to_all.16 = f32[16,1,1024]{2,1,0:T(1,128)S(1)} all-to-all(f32[16,1,1024]{2,1,0:T(1,128)S(1)} %broadcast_in_dim.29), channel_id=1, replica_groups=mesh['occ'=16,'ao'=16] {'ao'}, dimensions={0} | all-to-all | bytes 131072 | tf_op jit(solution)/shard_map/all_to_all | solution.py:9
  418.2 0.1 reduce_sum.18
  418.2 0.0 copy-done.2
  418.2 0.3 fusion
  418.5 20.4 %all_to_all.17 = f32[16,64,128]{2,1,0:T(8,128)S(1)} all-to-all(f32[16,64,128]{2,1,0:T(8,128)S(1)} %broadcast_in_dim.30), channel_id=1, replica_groups=mesh['occ'=16,'ao'=16] {'occ'}, dimensions={0} | all-to-all | bytes 1048576 | tf_op jit(solution)/shard_map/all_to_all | solution.py:9
  438.9 0.6 reduce_sum.19
  439.6 119.4 %reduce-scatter.2.cloned.1.call-done = f32[512,512]{1,0:T(8,128)} async-done(((f32[512,8192]{1,0:T(8,128)}), f32[512,512]{1,0:T(8,128)}) %reduce-scatter.2.cloned.1.call-update) | async-done | bytes 1048592 | tf_op jit(solution)/shard_map/reduce_scatter | solution.py:46
  (3 shorter events, 0.1 us)
Async XLA Ops:
  7.2 1.6 copy-start
  7.2 551.8 %reduce-scatter.2.cloned.1.call-start = ((), (), s32[]{:S(2)}) async-start(), calls=%async_computation.4 | async-start | bytes 17825792 | tf_op jit(solution)/shard_map/reduce_scatter | solution.py:46
  403.9 0.7 copy-start.1
  403.9 14.3 %copy-start.2 = (s32[1,8]{1,0:T(1,128)S(1)}, s32[1,8]{1,0:T(1,128)}, u32[]{:S(2)}) copy-start(s32[1,8]{1,0:T(1,128)} %param.8) | copy-start | bytes 100
Sparse Core Ops, SparseCore 0:
  404.0 154.9 reduce-scatter.1
